TPU v7x, 32 devices: a whole 2x2x4 slice. The times are simulated.
32 devices in a mesh: beam: 2 (over y), inp: 8 (over z, x), span: 2 (over core).
Axes of the slice: x: 2, y: 2, z: 4, core: 2. Of those that a mesh axis runs over, the one named last changes fastest.
Arguments:
- voltages: bfloat16 [2, 8, 1024, 16384], P(None, 'beam', 'inp', 'span'), parts along dimension 1, may hold values from -6 to 6
- gains: float32 [2, 8, 1024, 32], P(None, 'beam', 'inp'), parts along dimension 1, may hold values from -4 to 4
Outputs:
- visibilities: bfloat16 [256, 1024, 1024], P(('beam', 'inp'), 'span'), parts along dimension 0
There are 2 independent parts, one for each index of `beam`. A program takes and returns all parts, laid end to end along the dimension named above; each array names one. Nothing has to cross between parts.
All inputs are finite; a program needn't handle non-finite values.
Results may differ from a plain program's by a relative error of at most 0.0085.
Values may be sent and summed in bfloat16 or wider, within the bound.
A program may use at most 192 MiB of HBM per device.

v0:
```python
import math
import jax
import jax.numpy as jnp
from jax import lax
from jax.sharding import PartitionSpec as P

FINE = 32
TAPS = 4


def prototype(tap_count, fine_count):
    length = tap_count * fine_count
    offsets = jnp.arange(length).astype(jnp.float32)
    shifted = (offsets - length / 2 + 0.5) / fine_count
    taper = 0.5 - 0.5 * jnp.cos(2.0 * math.pi * (offsets + 0.5) / length)
    window = jnp.sinc(shifted) * taper
    window = window / jnp.sqrt(jnp.sum(window * window))
    return window.reshape(tap_count, fine_count)


def kernels(window, fine_count):
    points = jnp.arange(fine_count)
    phase_steps = points[:, None] * points[None, :] % fine_count
    angles = 2.0 * math.pi * phase_steps.astype(jnp.float32) / fine_count
    cosine = jnp.cos(angles)
    sine_part = jnp.sin(angles)
    result = []
    for tap_index in range(window.shape[0]):
        weights = window[tap_index][:, None]
        hcos = weights * cosine
        hsin = weights * sine_part
        result.append(jnp.stack([jnp.stack([hcos, -hsin]), jnp.stack([hsin, hcos])]))
    return jnp.stack(result)


def packed_rows(left_rows, right_rows, left_all, row_start):
    real_sums = jnp.einsum("cif,cjf->cij", left_rows, left_all, preferred_element_type=jnp.float32)
    imag_sums = jnp.einsum("cif,cjf->cij", right_rows, left_all, preferred_element_type=jnp.float32)
    row_index = row_start + jnp.arange(left_rows.shape[1])
    col_index = jnp.arange(left_all.shape[1])
    upper = row_index[:, None] <= col_index[None, :]
    return jnp.where(upper[None], real_sums, imag_sums)


def local(voltages, gains):
    coarse = voltages.shape[1]
    local_inputs = voltages.shape[2]
    samples = voltages.shape[3]
    frames = samples // FINE
    window = prototype(TAPS, FINE)
    filters = kernels(window, FINE)
    filter_table = jnp.transpose(filters, (1, 0, 3, 2, 4))
    filter_high = filter_table.astype(jnp.bfloat16)
    filter_low = (filter_table - filter_high.astype(jnp.float32)).astype(jnp.bfloat16)
    padded = jnp.pad(voltages, ((0, 0), (0, 0), (0, 0), (0, (TAPS - 1) * FINE)))
    stacked = jnp.stack(
        [padded[..., tap_index * FINE : tap_index * FINE + samples] for tap_index in range(TAPS)],
        axis=1,
    )
    stacked = stacked.reshape(2, TAPS, coarse, local_inputs, frames, FINE)
    spectra = jnp.einsum(
        "atcnmp,atpbk->bcknm", stacked, filter_high, preferred_element_type=jnp.float32
    )
    spectra = spectra + jnp.einsum(
        "atcnmp,atpbk->bcknm", stacked, filter_low, preferred_element_type=jnp.float32
    )
    gain_real = jnp.swapaxes(gains[0], 1, 2)[:, :, :, None]
    gain_imag = jnp.swapaxes(gains[1], 1, 2)[:, :, :, None]
    real_part = spectra[0] * gain_real - spectra[1] * gain_imag
    imag_part = spectra[0] * gain_imag + spectra[1] * gain_real
    outgoing = jnp.stack([real_part, imag_part]).astype(jnp.bfloat16)
    outgoing = outgoing.reshape(2, coarse * FINE, local_inputs, frames)
    turned = lax.all_to_all(outgoing, "inp", split_axis=1, concat_axis=2, tiled=True)
    inputs = turned.shape[2]
    span_count = lax.axis_size("span")
    row_count = inputs // span_count
    frame_scale = 1.0 / (span_count * frames)
    row_start = lax.axis_index("span") * row_count
    frame_piece = lax.all_gather(turned, "span", axis=3, tiled=True)
    left_all = jnp.concatenate([frame_piece[0], frame_piece[1]], axis=-1)
    own_rows = lax.dynamic_slice_in_dim(frame_piece, row_start, row_count, 2)
    left_rows = jnp.concatenate([own_rows[0], own_rows[1]], axis=-1)
    right_rows = jnp.concatenate([own_rows[1], -own_rows[0]], axis=-1)
    summed = packed_rows(left_rows, right_rows, left_all, row_start) * frame_scale
    return summed.astype(jnp.bfloat16)


def solution(mesh):
    placed = (P(None, "beam", "inp", "span"), P(None, "beam", "inp", None))
    return jax.shard_map(
        local,
        mesh=mesh,
        in_specs=placed,
        out_specs=P(("beam", "inp"), "span", None),
        check_vma=False,
    )
```

profile of v0, /device:TPU:0, one launch (start us, length us, event | category | flops | bytes accessed | tf_op | source)
XLA Modules:
  0.0 864.3 jit_solution(2377499240589222631)
XLA Ops:
  6.5 0.7 multiply_reduce_fusion
  8.0 21.2 %copy.28 = bf16[2,4,128,8192]{2,3,1,0:T(8,128)(2,1)} copy(bf16[2,4,128,8192]{3,2,1,0:T(8,128)(2,1)} %param.2) | data formatting | bytes 33554432 | tf_op args[0]
  29.2 32.5 %pad_slice_fusion.2 = (bf16[2,4,128,8192]{2,3,1,0:T(8,128)(2,1)}, bf16[2,4,128,8192]{2,3,1,0:T(8,128)(2,1)}, bf16[2,4,128,8192]{2,3,1,0:T(8,128)(2,1)}) fusion(bf16[2,4,128,8192]{2,3,1,0:T(8,128)(2,1)} %copy.28), kind=kLoop, calls=%fused_computation.22 | loop fusion | bytes 67108864 | tf_op jit(solution)/shard_map/slice | solution.py:57
  61.6 30.6 %copy.31 = bf16[2,1,4,128,256,32]{4,5,1,0,3,2:T(8,128)(2,1)} copy(bf16[2,1,4,128,256,32]{3,5,4,2,0,1:T(8,128)(2,1)} %bitcast.137) | data formatting | bytes 33554432 | tf_op jit(solution)/shard_map/stack | solution.py:56
  92.3 30.7 %copy.32 = bf16[2,1,4,128,256,32]{4,5,1,0,3,2:T(8,128)(2,1)} copy(bf16[2,1,4,128,256,32]{3,5,4,2,0,1:T(8,128)(2,1)} %bitcast.136) | data formatting | bytes 33554432 | tf_op jit(solution)/shard_map/stack | solution.py:56
  122.9 30.7 %copy.33 = bf16[2,1,4,128,256,32]{4,5,1,0,3,2:T(8,128)(2,1)} copy(bf16[2,1,4,128,256,32]{3,5,4,2,0,1:T(8,128)(2,1)} %bitcast.135) | data formatting | bytes 33554432 | tf_op jit(solution)/shard_map/stack | solution.py:56
  153.6 30.7 %copy.30 = bf16[2,1,4,128,256,32]{4,5,1,0,3,2:T(8,128)(2,1)} copy(bf16[2,1,4,128,256,32]{3,5,4,2,0,1:T(8,128)(2,1)} %bitcast.132) | data formatting | bytes 33554432 | tf_op jit(solution)/shard_map/stack | solution.py:56
  184.6 36.7 %fusion.1 = f32[2,32,4,128,256,1,1]{4,1,6,5,3,2,0:T(8,128)} fusion(bf16[2,1,4,128,256,32]{4,5,1,0,3,2:T(8,128)(2,1)} %copy.33, bf16[2,1,4,128,256,32]{4,5,1,0,3,2:T(8,128)(2,1)} %copy.32, bf16[2,1,4,128,256,32]{4,5,1,0,3,2:T(8,128)(2,1)} %copy.31, bf16[2,1,4,128,256,32]{4,5,1,0,3,2:T(8,128)(2,1)} %copy.30, ...), kind=kOutput, calls=%fused_computation.5 | convolution fusion | flops 4563521536 | bytes 100728832 | tf_op jit(solution)/shard_map/atcnmp,atpbk->bcknm/dot_general | solution.py:64
  221.2 44.4 %fusion = f32[2,4,32,128,256]{4,2,3,1,0:T(8,128)} fusion(f32[2,32,4,128,256,1,1]{4,1,6,5,3,2,0:T(8,128)} %fusion.1, bf16[2,1,4,128,256,32]{4,5,1,0,3,2:T(8,128)(2,1)} %copy.33, bf16[2,1,4,128,256,32]{4,5,1,0,3,2:T(8,128)(2,1)} %copy.32, bf16[2,1,4,128,256,32]{4,5,1,0,3,2:T(8,128)(2,1)} %copy.31, bf16[2,1,4,128,256,32]{4,5,1,0,3,2:T(8,128)(2,1)} %copy.30, ...), kind=kOutput, calls=%fused_computation.3 | convolution fusion | flops 4571926528 | bytes 134283264 | tf_op jit(solution)/shard_map/atcnmp,atpbk->bcknm/dot_general | solution.py:61
  265.7 0.1 copy.34
  265.9 17.8 %subtract_convert_fusion = (bf16[1,4,32,128,256]{4,2,3,1,0:T(8,128)(2,1)}, bf16[1,4,32,128,256]{4,2,3,1,0:T(8,128)(2,1)}) fusion(f32[2,4,32,128,256]{4,2,3,1,0:T(8,128)} %fusion, f32[4,32,128]{1,2,0:T(8,128)S(1)} %copy.35, f32[4,32,128]{1,2,0:T(8,128)S(1)} %copy.34), kind=kLoop, calls=%fused_computation.19 | loop fusion | flops 33554432 | bytes 50462720 | tf_op jit(solution)/shard_map/convert.3
  283.8 11.5 %copy.36 = bf16[1,4,32,128,256]{4,3,2,1,0:T(8,128)(2,1)} copy(bf16[1,4,32,128,256]{4,2,3,1,0:T(8,128)(2,1)} %get-tuple-element.7) | data formatting | bytes 16777216 | tf_op jit(solution)/shard_map/convert.3
  295.2 11.6 %copy.37 = bf16[1,4,32,128,256]{4,3,2,1,0:T(8,128)(2,1)} copy(bf16[1,4,32,128,256]{4,2,3,1,0:T(8,128)(2,1)} %get-tuple-element.8) | data formatting | bytes 16777216 | tf_op jit(solution)/shard_map/convert.2
  306.9 8.0 pad_maximum_fusion.3
  314.9 2.0 copy.38
  316.9 369.9 %all_to_all.18 = bf16[2,128,128,256]{3,2,0,1:T(8,128)(2,1)S(1)} all-to-all(bf16[2,128,128,256]{3,2,0,1:T(8,128)(2,1)S(1)} %copy.38), channel_id=1, replica_groups=mesh['beam'=2,'inp'=8,'span'=2] {'inp'}, dimensions={1} | all-to-all | bytes 33554432 | tf_op jit(solution)/shard_map/all_to_all | solution.py:73
  686.8 6.5 copy.40
  693.3 0.4 iota_compare_fusion
  693.7 49.8 %all-gather.2.cloned.1.call-done = bf16[2,16,1024,512]{3,2,1,0:T(8,128)(2,1)} async-done(((bf16[2,16,1024,256]{3,2,1,0:T(8,128)(2,1)}), bf16[2,16,1024,512]{3,2,1,0:T(8,128)(2,1)}) %all-gather.2.cloned.1.call-update) | async-done | bytes 33554448 | tf_op jit(solution)/shard_map/all_gather | solution.py:79
  743.5 22.5 %slice_bitcast_fusion.1 = (bf16[16,1024,512]{2,1,0:T(8,128)(2,1)}, bf16[16,1024,512]{2,1,0:T(8,128)(2,1)}) fusion(bf16[2,16,1024,512]{3,2,1,0:T(8,128)(2,1)} %all-gather.2.cloned.1.call-done), kind=kLoop, calls=%fused_computation.10 | loop fusion | bytes 67108864 | tf_op jit(solution)/shard_map/squeeze | solution.py:80
  765.9 10.3 %fusion.44 = (bf16[16,512,512]{2,1,0:T(8,128)(2,1)}, bf16[16,512,512]{2,1,0:T(8,128)(2,1)}) fusion(bf16[2,16,1024,512]{3,2,1,0:T(8,128)(2,1)} %all-gather.2.cloned.1.call-done, s32[]{:T(128)S(6)} %select_n.117), kind=kLoop, calls=%fused_computation.91 | loop fusion | flops 12582912 | bytes 25165828 | tf_op jit(solution)/shard_map/neg | solution.py:83
  776.2 7.4 dynamic-slice_bitcast_fusion
  783.6 36.8 %fusion.3 = f32[16,512,1024]{2,1,0:T(8,128)} fusion(bf16[16,1024,512]{2,1,0:T(8,128)(2,1)} %get-tuple-element.10, bf16[16,1024,512]{2,1,0:T(8,128)(2,1)} %get-tuple-element.9, bf16[16,512,512]{2,1,0:T(8,128)(2,1)} %get-tuple-element.5, bf16[16,512,512]{2,1,0:T(8,128)(2,1)} %dynamic-slice_bitcast_fusion), kind=kOutput, calls=%fused_computation.7 | convolution fusion | flops 17280532480 | bytes 83886080 | tf_op jit(solution)/shard_map/cif,cjf->cij/dot_general | solution.py:38
  820.5 37.0 %multiply_convert_fusion = bf16[16,512,1024]{2,1,0:T(8,128)(2,1)} fusion(f32[16,512,1024]{2,1,0:T(8,128)} %fusion.3, pred[512,1024]{1,0:T(8,128)(4,1)S(1)} %iota_compare_fusion, bf16[16,1024,512]{2,1,0:T(8,128)(2,1)} %get-tuple-element.10, bf16[16,1024,512]{2,1,0:T(8,128)(2,1)} %get-tuple-element.9, bf16[16,512,512]{2,1,0:T(8,128)(2,1)} %dynamic-slice_bitcast_fusion, ...), kind=kOutput, calls=%fused_computation.4 | convolution fusion | flops 17305698304 | bytes 101187584 | tf_op jit(solution)/shard_map/cif,cjf->cij/dot_general | solution.py:37
  (18 shorter events, 0.5 us)
Async XLA Ops:
  6.5 736.9 %all-gather.2.cloned.1.call-start = ((), (), s32[]{:S(2)}) async-start(), calls=%async_computation.1 | async-start | bytes 50331648 | tf_op jit(solution)/shard_map/all_gather | solution.py:79
  221.2 44.4 %copy-start = (f32[2,4,128,32]{2,3,1,0:T(8,128)S(1)}, f32[2,4,128,32]{2,3,1,0:T(8,128)}, u32[]{:S(2)}) copy-start(f32[2,4,128,32]{2,3,1,0:T(8,128)} %param.3) | copy-start | bytes 393220
Sparse Core Ops, SparseCore 0:
  693.4 49.9 all-gather.1
where the time goes:
time: 868 us; the launch traced here: 864 us
  blocking collectives  370 us (43%)
  local copies, waits for them, and re-layouts  238 us (27%)
  matrix products  155 us (18%)
  waiting for transfers between devices  49.8 us (6%)
  other arithmetic  37.4 us (4%)
  between operations  14.2 us (2%)
    all_to_all x1, blocking collectives, local(): lax.all_to_all(outgoing, 'inp', split_axis=1, concat_axis=2, tiled=True)  370 us
    another operation x4, local copies, waits for them, and re-layouts, local(): jnp.stack([padded[..., tap_index * FINE:tap_index * FINE + samples] for t...  123 us
    all_gather x1, waiting for transfers between devices, local(): frame_piece = lax.all_gather(turned, 'span', axis=3, tiled=True)  49.8 us
    dot_general x1, matrix products, local(): jnp.einsum('atcnmp,atpbk->bcknm', stacked, filter_high, preferred_element...  44.4 us
    dot_general x1, matrix products, packed_rows(): jnp.einsum('cif,cjf->cij', left_rows, left_all, preferred_element_type=jn...  37 us
    dot_general x1, matrix products, packed_rows(): jnp.einsum('cif,cjf->cij', right_rows, left_all, preferred_element_type=j...  36.8 us
    dot_general x1, matrix products, local(): jnp.einsum('atcnmp,atpbk->bcknm', stacked, filter_low, preferred_element_...  36.7 us
    slice x1, local copies, waits for them, and re-layouts, local(): padded[..., tap_index * FINE:tap_index * FINE + samples]  32.5 us
  transfers between devices with their start and end apart: 1, of which 1 were waited for; matrix products, arithmetic and copies ran while one was open for 0% of the time, Pallas kernels for 0%

commit v1 on v0

--- a/solution.py
+++ b/solution.py
@@ -6,6 +6,20 @@
 
 FINE = 32
 TAPS = 4
+
+
+def _change_levels_all(v0, pos_dim, z):
+    vec_out = v0.shape
+    response = v0.reshape(*vec_out[:pos_dim], z, vec_out[pos_dim] // z, *vec_out[pos_dim + 1 :])
+    arr_out = jnp.moveaxis(response, pos_dim, 0)
+    return arr_out
+
+
+def _choose_keys(array_in, on_dim):
+    z2 = list(array_in.shape[1:])
+    z2[on_dim] *= array_in.shape[0]
+    piece_now = jnp.moveaxis(array_in, 0, on_dim).reshape(z2)
+    return piece_now
 
 
 def prototype(tap_count, fine_count):
@@ -70,7 +84,19 @@
     imag_part = spectra[0] * gain_imag + spectra[1] * gain_real
     outgoing = jnp.stack([real_part, imag_part]).astype(jnp.bfloat16)
     outgoing = outgoing.reshape(2, coarse * FINE, local_inputs, frames)
-    turned = lax.all_to_all(outgoing, "inp", split_axis=1, concat_axis=2, tiled=True)
+
+    def manage_blocks(point, ax_name, page, a0):
+        last, tile_out = (lax.psum(1, ax_name), lax.axis_index(ax_name))
+        r_now = _change_levels_all(point, page, last)
+        kept_rows = [r_now[tile_out]]
+        for j0 in range(1, last):
+            carry_in = r_now[tile_out ^ j0]
+            kept_rows.append(lax.ppermute(carry_in, ax_name, [(s, s ^ j0) for s in range(last)]))
+        r_now = jnp.stack(kept_rows, axis=0)[tile_out ^ jnp.arange(last)]
+        row_out = _choose_keys(r_now, a0)
+        return row_out
+
+    turned = manage_blocks(outgoing, "inp", 1, 2)
     inputs = turned.shape[2]
     span_count = lax.axis_size("span")
     row_count = inputs // span_count

time: 868 us -> 897 us (1.033)
  blocking collectives: 370 us -> 0 us
  waiting for transfers between devices: 49.8 us -> 389 us
  local copies, waits for them, and re-layouts: 238 us -> 270 us
  starting transfers between devices: 0.01 us -> 13.8 us
  other arithmetic: 37.4 us -> 50.8 us
    all_to_all x1 -> x0, blocking collectives: 370 us -> none  [local(): lax.all_to_all(outgoing, 'inp', split_axis=1, concat_axis=2, tiled=True)]
    ppermute x0 -> x7, waiting for transfers between devices: none -> 255 us  [manage_blocks(): lax.ppermute(carry_in, ax_name, [(s, s ^ j0) for s in range(last)])]
    all_gather x1, waiting for transfers between devices: 49.8 us -> 134 us  [local(): frame_piece = lax.all_gather(turned, 'span', axis=3, tiled=True)]
    gather x0 -> x3, local copies, waits for them, and re-layouts: none -> 23.4 us  [manage_blocks(): r_now = jnp.stack(kept_rows, axis=0)[tile_out ^ jnp.arange(last)]]
    ppermute x0 -> x7, starting transfers between devices: none -> 13.7 us  [manage_blocks(): lax.ppermute(carry_in, ax_name, [(s, s ^ j0) for s in range(last)])]
    squeeze x0 -> x2, other arithmetic: none -> 11.3 us  [manage_blocks(): carry_in = r_now[tile_out ^ j0]]
    unnamed x3 -> x9, local copies, waits for them, and re-layouts: 21.2 us -> 32 us
    another operation x2 -> x1, other arithmetic: 25.8 us -> 17.9 us
  transfers between devices with their start and end apart: 1 -> 8, of which waited for: 1 -> 5; matrix products, arithmetic and copies ran while one was open for 0% -> 2% of each run, Pallas kernels for 0% -> 0%
where the time goes in v1:
time: 897 us; the launch traced here: 893 us
  waiting for transfers between devices  389 us (43%)
  local copies, waits for them, and re-layouts  270 us (30%)
  matrix products  155 us (17%)
  other arithmetic  50.8 us (6%)
  between operations  14.3 us (2%)
  starting transfers between devices  13.8 us (2%)
    ppermute x7, waiting for transfers between devices, manage_blocks(): lax.ppermute(carry_in, ax_name, [(s, s ^ j0) for s in range(last)])  255 us
    all_gather x1, waiting for transfers between devices, local(): frame_piece = lax.all_gather(turned, 'span', axis=3, tiled=True)  134 us
    another operation x4, local copies, waits for them, and re-layouts, local(): jnp.stack([padded[..., tap_index * FINE:tap_index * FINE + samples] for t...  123 us
    dot_general x1, matrix products, local(): jnp.einsum('atcnmp,atpbk->bcknm', stacked, filter_high, preferred_element...  44.4 us
    dot_general x1, matrix products, packed_rows(): jnp.einsum('cif,cjf->cij', left_rows, left_all, preferred_element_type=jn...  36.9 us
    dot_general x1, matrix products, packed_rows(): jnp.einsum('cif,cjf->cij', right_rows, left_all, preferred_element_type=j...  36.9 us
    dot_general x1, matrix products, local(): jnp.einsum('atcnmp,atpbk->bcknm', stacked, filter_low, preferred_element_...  36.7 us
    slice x1, local copies, waits for them, and re-layouts, local(): padded[..., tap_index * FINE:tap_index * FINE + samples]  32.5 us
  transfers between devices with their start and end apart: 8, of which 5 were waited for; matrix products, arithmetic and copies ran while one was open for 2% of the time, Pallas kernels for 0%

profile of v1, /device:TPU:0, one launch (start us, length us, event | category | flops | bytes accessed | tf_op | source)
XLA Modules:
  0.0 893.2 jit_solution(10771357685623179973)
XLA Ops:
  8.0 21.2 %copy.13 = bf16[2,4,128,8192]{2,3,1,0:T(8,128)(2,1)} copy(bf16[2,4,128,8192]{3,2,1,0:T(8,128)(2,1)} %param.2) | data formatting | bytes 33554432 | tf_op args[0]
  29.2 32.5 %pad_slice_fusion.2 = (bf16[2,4,128,8192]{2,3,1,0:T(8,128)(2,1)}, bf16[2,4,128,8192]{2,3,1,0:T(8,128)(2,1)}, bf16[2,4,128,8192]{2,3,1,0:T(8,128)(2,1)}) fusion(bf16[2,4,128,8192]{2,3,1,0:T(8,128)(2,1)} %copy.13), kind=kLoop, calls=%fused_computation.40 | loop fusion | bytes 67108864 | tf_op jit(solution)/shard_map/slice | solution.py:71
  61.7 30.6 %copy.16 = bf16[2,1,4,128,256,32]{4,5,1,0,3,2:T(8,128)(2,1)} copy(bf16[2,1,4,128,256,32]{3,5,4,2,0,1:T(8,128)(2,1)} %bitcast.173) | data formatting | bytes 33554432 | tf_op jit(solution)/shard_map/stack | solution.py:70
  92.3 30.7 %copy.17 = bf16[2,1,4,128,256,32]{4,5,1,0,3,2:T(8,128)(2,1)} copy(bf16[2,1,4,128,256,32]{3,5,4,2,0,1:T(8,128)(2,1)} %bitcast.172) | data formatting | bytes 33554432 | tf_op jit(solution)/shard_map/stack | solution.py:70
  123.0 30.6 %copy.18 = bf16[2,1,4,128,256,32]{4,5,1,0,3,2:T(8,128)(2,1)} copy(bf16[2,1,4,128,256,32]{3,5,4,2,0,1:T(8,128)(2,1)} %bitcast.171) | data formatting | bytes 33554432 | tf_op jit(solution)/shard_map/stack | solution.py:70
  153.6 30.6 %copy.15 = bf16[2,1,4,128,256,32]{4,5,1,0,3,2:T(8,128)(2,1)} copy(bf16[2,1,4,128,256,32]{3,5,4,2,0,1:T(8,128)(2,1)} %bitcast.163) | data formatting | bytes 33554432 | tf_op jit(solution)/shard_map/stack | solution.py:70
  184.6 36.7 %fusion.1 = f32[2,32,4,128,256,1,1]{4,1,6,5,3,2,0:T(8,128)} fusion(bf16[2,1,4,128,256,32]{4,5,1,0,3,2:T(8,128)(2,1)} %copy.18, bf16[2,1,4,128,256,32]{4,5,1,0,3,2:T(8,128)(2,1)} %copy.17, bf16[2,1,4,128,256,32]{4,5,1,0,3,2:T(8,128)(2,1)} %copy.16, bf16[2,1,4,128,256,32]{4,5,1,0,3,2:T(8,128)(2,1)} %copy.15, ...), kind=kOutput, calls=%fused_computation.23 | convolution fusion | flops 4563521536 | bytes 100728832 | tf_op jit(solution)/shard_map/atcnmp,atpbk->bcknm/dot_general | solution.py:78
  221.3 44.4 %fusion = f32[2,4,32,128,256]{4,2,3,1,0:T(8,128)} fusion(f32[2,32,4,128,256,1,1]{4,1,6,5,3,2,0:T(8,128)} %fusion.1, bf16[2,1,4,128,256,32]{4,5,1,0,3,2:T(8,128)(2,1)} %copy.18, bf16[2,1,4,128,256,32]{4,5,1,0,3,2:T(8,128)(2,1)} %copy.17, bf16[2,1,4,128,256,32]{4,5,1,0,3,2:T(8,128)(2,1)} %copy.16, bf16[2,1,4,128,256,32]{4,5,1,0,3,2:T(8,128)(2,1)} %copy.15, ...), kind=kOutput, calls=%fused_computation.5 | convolution fusion | flops 4571926528 | bytes 134283264 | tf_op jit(solution)/shard_map/atcnmp,atpbk->bcknm/dot_general | solution.py:75
  266.0 17.9 %subtract_convert_fusion = (bf16[1,4,32,128,256]{4,2,3,1,0:T(8,128)(2,1)}, bf16[1,4,32,128,256]{4,2,3,1,0:T(8,128)(2,1)}) fusion(f32[2,4,32,128,256]{4,2,3,1,0:T(8,128)} %fusion, f32[4,32,128]{1,2,0:T(8,128)S(1)} %copy.20, f32[4,32,128]{1,2,0:T(8,128)S(1)} %copy.19), kind=kLoop, calls=%fused_computation.37 | loop fusion | flops 33554432 | bytes 50462720 | tf_op jit(solution)/shard_map/convert.3
  283.8 11.5 %copy.21 = bf16[1,4,32,128,256]{4,3,2,1,0:T(8,128)(2,1)} copy(bf16[1,4,32,128,256]{4,2,3,1,0:T(8,128)(2,1)} %get-tuple-element.7) | data formatting | bytes 16777216 | tf_op jit(solution)/shard_map/convert.3
  295.3 11.6 %copy.22 = bf16[1,4,32,128,256]{4,3,2,1,0:T(8,128)(2,1)} copy(bf16[1,4,32,128,256]{4,2,3,1,0:T(8,128)(2,1)} %get-tuple-element.8) | data formatting | bytes 16777216 | tf_op jit(solution)/shard_map/convert.2
  307.0 8.2 fusion.27
  327.1 37.1 %collective-permute-done = bf16[2,16,128,256]{3,2,1,0:T(8,128)(2,1)} collective-permute-done((bf16[2,16,128,256]{3,2,1,0:T(8,128)(2,1)}, bf16[2,16,128,256]{3,2,1,0:T(8,128)(2,1)}, u32[]{:S(2)}, u32[]{:S(2)}) %collective-permute-start) | collective-permute-done | bytes 2097184 | tf_op jit(solution)/shard_map/ppermute | solution.py:94
  369.8 86.2 %collective-permute-done.1 = bf16[2,16,128,256]{3,2,1,0:T(8,128)(2,1)} collective-permute-done((bf16[2,16,128,256]{3,2,1,0:T(8,128)(2,1)}, bf16[2,16,128,256]{3,2,1,0:T(8,128)(2,1)}, u32[]{:S(2)}, u32[]{:S(2)}) %collective-permute-start.1) | collective-permute-done | bytes 2097184 | tf_op jit(solution)/shard_map/ppermute | solution.py:94
  460.7 38.0 %collective-permute-done.2 = bf16[2,16,128,256]{3,2,1,0:T(8,128)(2,1)} collective-permute-done((bf16[2,16,128,256]{3,2,1,0:T(8,128)(2,1)}, bf16[2,16,128,256]{3,2,1,0:T(8,128)(2,1)}, u32[]{:S(2)}, u32[]{:S(2)}) %collective-permute-start.2) | collective-permute-done | bytes 2097184 | tf_op jit(solution)/shard_map/ppermute | solution.py:94
  502.3 93.3 %collective-permute-done.4 = bf16[2,16,128,256]{3,2,1,0:T(8,128)(2,1)} collective-permute-done((bf16[2,16,128,256]{3,2,1,0:T(8,128)(2,1)}, bf16[2,16,128,256]{3,2,1,0:T(8,128)(2,1)}, u32[]{:S(2)}, u32[]{:S(2)}) %collective-permute-start.4) | collective-permute-done | bytes 2097184 | tf_op jit(solution)/shard_map/ppermute | solution.py:94
  606.4 8.1 gather_fusion
  614.5 8.2 gather_fusion.1
  622.7 8.4 maximum_bitcast_fusion.5
  638.0 134.4 %all-gather.2.cloned.1.call-done = bf16[2,16,1024,512]{3,2,1,0:T(8,128)(2,1)} async-done(((bf16[2,16,1024,256]{3,2,1,0:T(8,128)(2,1)}), bf16[2,16,1024,512]{3,2,1,0:T(8,128)(2,1)}) %all-gather.2.cloned.1.call-update) | async-done | bytes 33554448 | tf_op jit(solution)/shard_map/all_gather | solution.py:105
  772.4 22.5 %slice_bitcast_fusion.1 = (bf16[16,1024,512]{2,1,0:T(8,128)(2,1)}, bf16[16,1024,512]{2,1,0:T(8,128)(2,1)}) fusion(bf16[2,16,1024,512]{3,2,1,0:T(8,128)(2,1)} %all-gather.2.cloned.1.call-done), kind=kLoop, calls=%fused_computation.28 | loop fusion | bytes 67108864 | tf_op jit(solution)/shard_map/squeeze | solution.py:106
  794.9 10.3 %fusion.60 = (bf16[16,512,512]{2,1,0:T(8,128)(2,1)}, bf16[16,512,512]{2,1,0:T(8,128)(2,1)}) fusion(bf16[2,16,1024,512]{3,2,1,0:T(8,128)(2,1)} %all-gather.2.cloned.1.call-done, s32[]{:T(128)S(6)} %select_n.160), kind=kLoop, calls=%fused_computation.135 | loop fusion | flops 12582912 | bytes 25165828 | tf_op jit(solution)/shard_map/neg | solution.py:109
  812.6 36.9 %fusion.3 = f32[16,512,1024]{2,1,0:T(8,128)} fusion(bf16[16,1024,512]{2,1,0:T(8,128)(2,1)} %get-tuple-element.10, bf16[16,1024,512]{2,1,0:T(8,128)(2,1)} %get-tuple-element.9, bf16[16,512,512]{2,1,0:T(8,128)(2,1)} %get-tuple-element.5, bf16[16,512,512]{2,1,0:T(8,128)(2,1)} %dynamic-slice_bitcast_fusion), kind=kOutput, calls=%fused_computation.25 | convolution fusion | flops 17280532480 | bytes 83886080 | tf_op jit(solution)/shard_map/cif,cjf->cij/dot_general | solution.py:52
  849.5 36.9 %multiply_convert_fusion = bf16[16,512,1024]{2,1,0:T(8,128)(2,1)} fusion(f32[16,512,1024]{2,1,0:T(8,128)} %fusion.3, pred[512,1024]{1,0:T(8,128)(4,1)S(1)} %iota_compare_fusion, bf16[16,1024,512]{2,1,0:T(8,128)(2,1)} %get-tuple-element.10, bf16[16,1024,512]{2,1,0:T(8,128)(2,1)} %get-tuple-element.9, bf16[16,512,512]{2,1,0:T(8,128)(2,1)} %dynamic-slice_bitcast_fusion, ...), kind=kOutput, calls=%fused_computation.6 | convolution fusion | flops 17305698304 | bytes 101187584 | tf_op jit(solution)/shard_map/cif,cjf->cij/dot_general | solution.py:51
  (45 shorter events, 52.2 us)
Async XLA Ops:
  6.5 765.9 %all-gather.2.cloned.1.call-start = ((), (), s32[]{:S(2)}) async-start(), calls=%async_computation | async-start | bytes 50331648 | tf_op jit(solution)/shard_map/all_gather | solution.py:105
  221.3 44.4 %copy-start = (f32[2,4,128,32]{2,3,1,0:T(8,128)S(1)}, f32[2,4,128,32]{2,3,1,0:T(8,128)}, u32[]{:S(2)}) copy-start(f32[2,4,128,32]{2,3,1,0:T(8,128)} %param.3) | copy-start | bytes 393220
  315.2 49.0 %collective-permute-start = (bf16[2,16,128,256]{3,2,1,0:T(8,128)(2,1)}, bf16[2,16,128,256]{3,2,1,0:T(8,128)(2,1)}, u32[]{:S(2)}, u32[]{:S(2)}) collective-permute-start(bf16[2,16,128,256]{3,2,1,0:T(8,128)(2,1)} %get-tuple-element.14), channel_id=1, source_target_pairs={{0,2},{2,0},{4,6},{6,4},{8,10},{10,8},{12,14},{14,12},{1,3},{3,1},... | collective-permute-start | bytes 6291464 | tf_op jit(solution)/shard_map/ppermute | solution.py:94
  318.2 137.8 %collective-permute-start.1 = (bf16[2,16,128,256]{3,2,1,0:T(8,128)(2,1)}, bf16[2,16,128,256]{3,2,1,0:T(8,128)(2,1)}, u32[]{:S(2)}, u32[]{:S(2)}) collective-permute-start(bf16[2,16,128,256]{3,2,1,0:T(8,128)(2,1)} %get-tuple-element.15), channel_id=1, source_target_pairs={{0,4},{2,6},{4,0},{6,2},{8,12},{10,14},{12,8},{14,10},{1,5},{3,7},... | collective-permute-start | bytes 6291464 | tf_op jit(solution)/shard_map/ppermute | solution.py:94
  319.8 178.9 %collective-permute-start.2 = (bf16[2,16,128,256]{3,2,1,0:T(8,128)(2,1)}, bf16[2,16,128,256]{3,2,1,0:T(8,128)(2,1)}, u32[]{:S(2)}, u32[]{:S(2)}) collective-permute-start(bf16[2,16,128,256]{3,2,1,0:T(8,128)(2,1)} %get-tuple-element.16), channel_id=1, source_target_pairs={{0,6},{2,4},{4,2},{6,0},{8,14},{10,12},{12,10},{14,8},{1,7},{3,5},... | collective-permute-start | bytes 6291464 | tf_op jit(solution)/shard_map/ppermute | solution.py:94
  319.8 180.7 %collective-permute-start.3 = (bf16[2,16,128,256]{3,2,1,0:T(8,128)(2,1)}, bf16[2,16,128,256]{3,2,1,0:T(8,128)(2,1)}, u32[]{:S(2)}, u32[]{:S(2)}) collective-permute-start(bf16[2,16,128,256]{3,2,1,0:T(8,128)(2,1)} %get-tuple-element.17), channel_id=1, source_target_pairs={{0,8},{2,10},{4,12},{6,14},{8,0},{10,2},{12,4},{14,6},{1,9},{3,11}... | collective-permute-start | bytes 6291464 | tf_op jit(solution)/shard_map/ppermute | solution.py:94
  322.8 272.8 %collective-permute-start.4 = (bf16[2,16,128,256]{3,2,1,0:T(8,128)(2,1)}, bf16[2,16,128,256]{3,2,1,0:T(8,128)(2,1)}, u32[]{:S(2)}, u32[]{:S(2)}) collective-permute-start(bf16[2,16,128,256]{3,2,1,0:T(8,128)(2,1)} %get-tuple-element.18), channel_id=1, source_target_pairs={{0,10},{2,8},{4,14},{6,12},{8,2},{10,0},{12,6},{14,4},{1,11},{3,9}... | collective-permute-start | bytes 6291464 | tf_op jit(solution)/shard_map/ppermute | solution.py:94
  364.2 233.2 %collective-permute-start.5 = (bf16[2,16,128,256]{3,2,1,0:T(8,128)(2,1)}, bf16[2,16,128,256]{3,2,1,0:T(8,128)(2,1)}, u32[]{:S(2)}, u32[]{:S(2)}) collective-permute-start(bf16[2,16,128,256]{3,2,1,0:T(8,128)(2,1)} %fusion.21), channel_id=1, source_target_pairs={{0,12},{2,14},{4,8},{6,10},{8,4},{10,6},{12,0},{14,2},{1,13},{3,15... | collective-permute-start | bytes 6291464 | tf_op jit(solution)/shard_map/ppermute | solution.py:94
  456.0 143.2 %collective-permute-start.6 = (bf16[2,16,128,256]{3,2,1,0:T(8,128)(2,1)S(1)}, bf16[2,16,128,256]{3,2,1,0:T(8,128)(2,1)S(1)}, u32[]{:S(2)}, u32[]{:S(2)}) collective-permute-start(bf16[2,16,128,256]{3,2,1,0:T(8,128)(2,1)S(1)} %get-tuple-element.13), channel_id=1, source_target_pairs={{0,14},{2,12},{4,10},{6,8},{8,6},{10,4},{12,2},{14,0},{1,15},{3,13... | collective-permute-start | bytes 6291464 | tf_op jit(solution)/shard_map/ppermute | solution.py:94
Sparse Core Ops, SparseCore 0:
  637.8 134.6 all-gather.1
